TPU v7x, 128 devices: a whole 4x4x4 slice. The times are simulated.
128 devices in a mesh: lon: 32 (over x, y, core), lat: 4 (over z).
Axes of the slice: x: 4, y: 4, z: 4, core: 2. Of those that a mesh axis runs over, the one named last changes fastest.
Arguments:
- vel_base: bfloat16 [32, 4, 8, 16, 2, 128], P('lon', 'lat'), may hold values from -1.25 to 1.25
- vel_grad: bfloat16 [32, 4, 8, 16, 4, 128], P('lon', 'lat'), may hold values from -0.29882812 to 0.29882812
- route_dev: int32 [32, 4, 8, 128, 1], P('lon', 'lat'), may hold values from 0 to 127; in each aligned block of 128 rows (0 to 127, 128 to 255, ..., all dimensions but the last counted through in order) at most 2 rows name the same one
- route_block: int32 [32, 4, 8, 128], P('lon', 'lat'), may hold values from 0 to 15
- seed_cells: int32 [8, 2048, 4096], P(None, 'lat', 'lon'), may hold values from 0 to 127
Outputs:
- flow_map: float32 [2, 2048, 4096], P(None, 'lat', 'lon')
- ftle_field: float32 [2048, 4096], P('lat', 'lon')
Inputs may be any that keep to these rules, and one draw needn't show every extreme that they name: `route_dev`: in each step, at most 2 of the 128 seed groups of one device name the same owner; in some steps of some devices an owner is named by exactly 2 groups.
All inputs are finite; a program needn't handle non-finite values.
Results may differ from a plain program's by a relative error of at most 0.0003.
Values may be sent and summed in bfloat16 or wider, within the bound.
A program may use at most 64 MiB of HBM per device.

v0:
```python
import jax
import jax.numpy as jnp
from jax import lax
from jax.experimental import pallas as pl
from jax.experimental.pallas import tpu as pltpu
from jax.sharding import PartitionSpec as P

MESH = pl.DeviceIdType.MESH
STEPS = 8
CHUNKS = 2
PER = STEPS // CHUNKS
GROUPS = 128
GROUP_ROWS = 4
BLOCKS = 16
WIDTH = 256
DIMS = ((1, 2, 0), (2, 0, 1), (0, 1, 2))


def owner_parts(owner):
    return (owner >> 5) & 3, (owner >> 3) & 3, owner & 3, (owner >> 2) & 1


def owner_number(place, core):
    return place[0] * 32 + place[1] * 8 + core * 4 + place[2]


def kernel(
    table_ref, dev_ref, block_ref, cells_hbm, flow_ref, ftle_ref,
    tab, rep, rcv, cells, pick, sort, ask, asked, first, state, coef,
    rows_out, rows_in, cols_out, cols_in,
    cell_sem, own_sem, back_sem, send1, recv1, send2, recv2, send3, recv3, sendq, recvq, sendh, recvh,
):
    lon = lax.axis_index("lon")
    lat = lax.axis_index("lat")
    core = lon % 2
    here = (lon // 8, (lon // 2) % 4, lat)
    n_lon = 32

    def device(place, which):
        return ((place[0] * 4 + place[1]) * 2 + which, place[2])

    def moved(dim, by):
        place = list(here)
        place[dim] = (place[dim] + by) % 4
        return place

    east, west = (lon + 1) % n_lon, (lon + n_lon - 1) % n_lon
    partners = [device(moved(dim, by), (core + flip) % 2) for dim in range(3) for by in (1, 2, 3) for flip in (0, 1)]
    partners += [device(here, 1 - core), (east, lat), (west, lat)]

    cells_copy = pltpu.make_async_copy(cells_hbm, cells, cell_sem)
    cells_copy.start()
    own = []
    for k, (d1, d2, _) in enumerate(DIMS):
        for c in range(CHUNKS):
            own.append(
                pltpu.make_async_copy(
                    table_ref.at[k, pl.ds(c * PER, PER)], tab.at[k, c, here[d2], here[d1]], own_sem.at[k, c]
                )
            )
            own[-1].start()

    barrier = pltpu.get_barrier_semaphore()
    for partner in partners:
        pl.semaphore_signal(barrier, inc=1, device_id=partner, device_id_type=MESH)
    pl.semaphore_wait(barrier, len(partners))

    def remote(src, dst, send, recv, target):
        return pltpu.make_async_remote_copy(
            src_ref=src, dst_ref=dst, send_sem=send, recv_sem=recv, device_id=target, device_id_type=MESH
        )

    phase1, phase2, phase3, query, back = {}, {}, {}, {}, {}
    for c in range(CHUNKS):
        for k, (d1, d2, d3) in enumerate(DIMS):
            for by in (1, 3, 2):
                phase1[k, c, by] = remote(
                    table_ref.at[k, pl.ds(c * PER, PER)], tab.at[k, c, here[d2], here[d1]],
                    send1.at[k, c, by - 1], recv1.at[k, c, by - 1], device(moved(d1, by), core),
                )
                phase2[k, c, by] = remote(
                    tab.at[k, c, here[d2]], tab.at[k, c, here[d2]],
                    send2.at[k, c, by - 1], recv2.at[k, c, by - 1], device(moved(d2, by), core),
                )
            mine = here[d3] * 2 + core
            for i, (by, flip) in enumerate(((1, 0), (3, 0), (2, 0), (1, 1), (3, 1), (2, 1), (0, 1))):
                place, which = moved(d3, by), (core + flip) % 2
                theirs = place[d3] * 2 + which
                phase3[k, c, i] = remote(
                    rep.at[k, c, theirs], rcv.at[k, c, mine], send3.at[k, c, i], recv3.at[k, c, i], device(place, which)
                )
                if c == 0:
                    query[k, i] = remote(
                        ask.at[k, theirs // 4], asked.at[k, mine], sendq.at[k, i], recvq.at[k, i], device(place, which)
                    )
            back[k, c] = pltpu.make_async_copy(rep.at[k, c, mine], rcv.at[k, c, mine], back_sem.at[k, c])

    for c in range(CHUNKS):
        for by in (1, 3, 2):
            for k in range(3):
                phase1[k, c, by].start()

    lane = lax.broadcasted_iota(jnp.int32, (GROUPS, 128), 1)
    group = lax.broadcasted_iota(jnp.int32, (GROUPS, 128), 0)
    dev_columns = jnp.transpose(dev_ref[...].astype(jnp.float32))
    block_columns = jnp.transpose(block_ref[...].astype(jnp.float32))
    lane_f, group_f = lane.astype(jnp.float32), group.astype(jnp.float32)
    for s in range(STEPS):
        named = jnp.broadcast_to(dev_columns[:, s : s + 1], (GROUPS, 128)) == lane_f
        value = group_f * BLOCKS + jnp.broadcast_to(block_columns[:, s : s + 1], (GROUPS, 128))
        last = jnp.max(jnp.where(named, value, -1.0), axis=0, keepdims=True)
        least = jnp.min(jnp.where(named, value, 1e6), axis=0, keepdims=True)
        first[0, s : s + 1, :] = jnp.where(last >= 0.0, last - BLOCKS * jnp.floor(last * (1.0 / BLOCKS)), -1e4)
        first[1, s : s + 1, :] = jnp.where(least < last, least - BLOCKS * jnp.floor(least * (1.0 / BLOCKS)), -1e4)
    wide = lax.broadcasted_iota(jnp.int32, (8, 128), 1)
    for k, (d1, d2, d3) in enumerate(DIMS):
        for half in range(2):
            place = [None] * 3
            number = wide + half * 128
            place[d1], place[d2], place[d3] = (number >> 1) & 3, (number >> 3) & 3, (number >> 6) & 3
            index = owner_number(place, (number >> 5) & 1)
            chosen = jnp.where(
                (number & 1) == 0,
                jnp.take_along_axis(first[0], index, axis=1, mode="promise_in_bounds"),
                jnp.take_along_axis(first[1], index, axis=1, mode="promise_in_bounds"),
            )
            ask[k, half] = chosen + (((number >> 1) & 15) * BLOCKS).astype(jnp.float32)
        for i in range(7):
            query[k, i].start()
        asked[k, here[d3] * 2 + core] = ask[k, here[d3] // 2]

    for c in range(CHUNKS):
        for k in range(3):
            own[k * CHUNKS + c].wait()
            for by in (1, 3, 2):
                phase1[k, c, by].wait_recv()
            for by in (1, 3, 2):
                phase2[k, c, by].start()

    dev_int = dev_columns.astype(jnp.int32)
    slot_lane = lax.broadcasted_iota(jnp.int32, (GROUPS, WIDTH), 1)
    for s in range(STEPS):
        same = (jnp.broadcast_to(dev_columns[:, s : s + 1], (GROUPS, 128)) == dev_ref[s : s + 1, :].astype(jnp.float32)) & (
            lane > group
        )
        rank = jnp.max(jnp.where(same, 1.0, 0.0), axis=1, keepdims=True).astype(jnp.int32)
        x, y, z, which = owner_parts(dev_int[:, s : s + 1])
        place = (x, y, z)
        for k, (d1, d2, d3) in enumerate(DIMS):
            slot = (((place[d3] * 2 + which) * 4 + place[d2]) * 4 + place[d1]) * 2 + rank
            sort[k, s] = jnp.where(jnp.broadcast_to(slot, (GROUPS, WIDTH)) == slot_lane, -1.0 / STEPS, 0.0).astype(jnp.bfloat16)

    block_lane = lax.broadcasted_iota(jnp.int32, (WIDTH, WIDTH), 1).astype(jnp.float32)
    for k, (_, _, d3) in enumerate(DIMS):
        for i in range(7):
            query[k, i].wait_recv()
        window = (here[d3] * 2 + core) % 4
        halves = []
        for half in range(2):
            total = jnp.full((8, 128), -1e4, jnp.float32)
            for r in range(4):
                turned = pltpu.roll(asked[k, half * 4 + r], (r - window + 4) % 4 * 32, 1)
                total = jnp.where(wide // 32 == r, turned, total)
            halves.append(jnp.transpose(total))
        rows = jnp.concatenate(halves, axis=0)
        for s in range(STEPS):
            pick[k, s] = jnp.where(
                jnp.broadcast_to(rows[:, s : s + 1], (WIDTH, WIDTH)) == block_lane, 1.0, 0.0
            ).astype(jnp.bfloat16)

    for c in range(CHUNKS):
        for k in range(3):
            for by in (1, 3, 2):
                phase2[k, c, by].wait_recv()

            @pl.loop(0, PER)
            def _(j):
                found = jnp.dot(
                    pick[k, c * PER + j], tab[k, c, :, :, j].reshape(WIDTH, WIDTH), preferred_element_type=jnp.float32
                )
                rep[k, c, :, j] = found.astype(jnp.bfloat16).reshape(8, 32, WIDTH)

            for i in range(7):
                phase3[k, c, i].start()
            back[k, c].start()

    state[...] = jnp.zeros_like(state)
    cells_copy.wait()
    for c in range(CHUNKS):
        for k in range(3):
            back[k, c].wait()
            for i in range(7):
                phase3[k, c, i].wait_recv()

        @pl.loop(0, PER)
        def _(j):
            step = c * PER + j
            for k in range(3):
                found = jnp.dot(
                    sort[k, step], rcv[k, c, :, j].reshape(WIDTH, WIDTH), preferred_element_type=jnp.float32
                )
                coef[2 * k] = found[:, :128]
                coef[2 * k + 1] = found[:, 128:]

            @pl.loop(0, GROUPS // 8)
            def _(t):
                start = pl.multiple_of(t * 8, 8)
                tables = [coef[m, pl.ds(start, 8), :] for m in range(6)]
                for q in range(GROUP_ROWS):
                    index = cells[step, pl.ds(t * 32 + q, 8, stride=GROUP_ROWS), :]
                    vx, vy, gxx, gxy, gyx, gyy = (
                        jnp.take_along_axis(table, index, axis=1, mode="promise_in_bounds") for table in tables
                    )
                    px, py = state[0, q, pl.ds(start, 8), :], state[1, q, pl.ds(start, 8), :]
                    kx = vx + (gxx * px + gxy * py)
                    ky = vy + (gyx * px + gyy * py)
                    wx, wy = kx, ky
                    for part in (0.25, 1.0 / 3.0, 0.5):
                        wx, wy = kx + part * (gxx * wx + gxy * wy), ky + part * (gyx * wx + gyy * wy)
                    state[0, q, pl.ds(start, 8), :] = px + wx
                    state[1, q, pl.ds(start, 8), :] = py + wy

    rows_out[...] = jnp.zeros_like(rows_out)
    cols_out[...] = jnp.zeros_like(cols_out)
    for comp in range(2):
        rows_out[comp : comp + 1, :] = state[comp, 0, 0:1, :]
        rows_out[2 + comp : 3 + comp, :] = state[comp, GROUP_ROWS - 1, GROUPS - 1 : GROUPS, :]
    halo = []
    for i, by in enumerate((1, 3)):
        halo.append(remote(rows_out, rows_in.at[i], sendh.at[i], recvh.at[i], device(moved(2, by), core)))
        halo[-1].start()
    for comp in range(2):
        for q in range(GROUP_ROWS):
            turned = jnp.transpose(state[comp, q])
            cols_out[q, comp : comp + 1, :] = turned[0:1, :]
            cols_out[q, 2 + comp : 3 + comp, :] = turned[127:128, :]
    for i, lon_to in enumerate((east, west)):
        halo.append(remote(cols_out, cols_in.at[i], sendh.at[2 + i], recvh.at[2 + i], (lon_to, lat)))
        halo[-1].start()
    for comp in range(2):
        for q in range(GROUP_ROWS):
            flow_ref[comp, pl.ds(q, GROUPS, stride=GROUP_ROWS), :] = state[comp, q]
    for copy in halo:
        copy.wait_recv()
    south_own, north_own = lat == 0, lat == 3
    at_west, at_east = lane == 0, lane == 127
    bottom, top = group == 0, group == GROUPS - 1
    diffs = {}
    for comp in range(2):
        south = jnp.where(south_own, rows_out[comp : comp + 1, :], rows_in[0, 2 + comp : 3 + comp, :])
        north = jnp.where(north_own, rows_out[2 + comp : 3 + comp, :], rows_in[1, comp : comp + 1, :])
        for q in range(GROUP_ROWS):
            own_rows = state[comp, q]
            west_column = jnp.transpose(cols_in[0, q])[:, 2 + comp : 3 + comp]
            east_column = jnp.transpose(cols_in[1, q])[:, comp : comp + 1]
            low = jnp.where(at_west, west_column, pltpu.roll(own_rows, 1, 1))
            high = jnp.where(at_east, east_column, pltpu.roll(own_rows, 127, 1))
            diffs[comp, q, 0] = (high - low) * 0.5
            if q == 0:
                below = jnp.where(bottom, south, pltpu.roll(state[comp, GROUP_ROWS - 1], 1, 0))
            else:
                below = state[comp, q - 1]
            if q == GROUP_ROWS - 1:
                above = jnp.where(top, north, pltpu.roll(state[comp, 0], GROUPS - 1, 0))
            else:
                above = state[comp, q + 1]
            diffs[comp, q, 1] = (above - below) * 0.5
    for q in range(GROUP_ROWS):
        map_xx, map_yx = 1.0 + diffs[0, q, 0], diffs[1, q, 0]
        map_xy, map_yy = diffs[0, q, 1], 1.0 + diffs[1, q, 1]
        green_xx = map_xx * map_xx + map_yx * map_yx
        green_yy = map_xy * map_xy + map_yy * map_yy
        green_xy = map_xx * map_xy + map_yx * map_yy
        half_diff = 0.5 * (green_xx - green_yy)
        largest = 0.5 * (green_xx + green_yy) + jnp.sqrt(half_diff * half_diff + green_xy * green_xy)
        ftle_ref[pl.ds(q, GROUPS, stride=GROUP_ROWS), :] = 0.5 * jnp.log(largest)

    for copies in (phase1, phase2, phase3, query):
        for copy in copies.values():
            copy.wait_send()
    for copy in halo:
        copy.wait_send()


def body(vel_base, vel_grad, route_dev, route_block, seed_cells):
    table = jnp.concatenate([vel_base[0, 0], vel_grad[0, 0]], axis=2).reshape(STEPS, BLOCKS, 3, WIDTH)
    table = jnp.transpose(table, (2, 0, 1, 3))
    dma = pltpu.SemaphoreType.DMA
    vmem = pl.BlockSpec(memory_space=pltpu.VMEM)
    return pl.pallas_call(
        kernel,
        out_shape=(
            jax.ShapeDtypeStruct((2, 512, 128), jnp.float32),
            jax.ShapeDtypeStruct((512, 128), jnp.float32),
        ),
        in_specs=[vmem, vmem, vmem, pl.BlockSpec(memory_space=pl.ANY)],
        out_specs=(vmem, vmem),
        scratch_shapes=[
            pltpu.VMEM((3, CHUNKS, 4, 4, PER, BLOCKS, WIDTH), jnp.bfloat16),
            pltpu.VMEM((3, CHUNKS, 8, PER, 32, WIDTH), jnp.bfloat16),
            pltpu.VMEM((3, CHUNKS, 8, PER, 32, WIDTH), jnp.bfloat16),
            pltpu.VMEM((STEPS, 512, 128), jnp.int32),
            pltpu.VMEM((3, STEPS, WIDTH, WIDTH), jnp.bfloat16),
            pltpu.VMEM((3, STEPS, GROUPS, WIDTH), jnp.bfloat16),
            pltpu.VMEM((3, 2, 8, 128), jnp.float32),
            pltpu.VMEM((3, 8, 8, 128), jnp.float32),
            pltpu.VMEM((2, STEPS, 128), jnp.float32),
            pltpu.VMEM((2, GROUP_ROWS, GROUPS, 128), jnp.float32),
            pltpu.VMEM((6, GROUPS, 128), jnp.float32),
            pltpu.VMEM((8, 128), jnp.float32),
            pltpu.VMEM((2, 8, 128), jnp.float32),
            pltpu.VMEM((GROUP_ROWS, 8, 128), jnp.float32),
            pltpu.VMEM((2, GROUP_ROWS, 8, 128), jnp.float32),
            dma, dma((3, CHUNKS)), dma((3, CHUNKS)),
            dma((3, CHUNKS, 3)), dma((3, CHUNKS, 3)),
            dma((3, CHUNKS, 3)), dma((3, CHUNKS, 3)),
            dma((3, CHUNKS, 7)), dma((3, CHUNKS, 7)),
            dma((3, 7)), dma((3, 7)),
            dma((4,)), dma((4,)),
        ],
        compiler_params=pltpu.CompilerParams(
            collective_id=0, has_side_effects=True, vmem_limit_bytes=48 << 20
        ),
    )(table, route_dev[0, 0, :, :, 0], route_block[0, 0], seed_cells)


def solution(mesh):
    in_specs = (
        P("lon", "lat", None, None, None, None),
        P("lon", "lat", None, None, None, None),
        P("lon", "lat", None, None, None),
        P("lon", "lat", None, None),
        P(None, "lat", "lon"),
    )
    out_specs = (P(None, "lat", "lon"), P("lat", "lon"))
    return jax.shard_map(body, mesh=mesh, in_specs=in_specs, out_specs=out_specs, check_vma=False)
```

profile of v0, /device:TPU:1, one launch (start us, length us, event | category | flops | bytes accessed | tf_op | source)
XLA Modules:
  0.0 63.4 jit_solution(12258327967227078687)
XLA Ops:
  0.6 1.0 %pad_maximum_fusion = bf16[8,16,6,128]{3,2,1,0:T(8,128)(2,1)S(1)} fusion(bf16[8,16,4,128]{3,2,1,0:T(4,128)(2,1)} %bitcast.10, bf16[8,16,2,128]{3,2,1,0:T(2,128)(2,1)} %bitcast.11), kind=kLoop, calls=%fused_computation | loop fusion | flops 393216 | bytes 393216 | tf_op jit(solution)/shard_map/concatenate | solution.py:286
  1.7 0.2 reshape.7
  1.9 0.0 copy-start
  1.9 1.6 %copy-done = s32[8,512,128]{2,1,0:T(8,128)S(1)} copy-done((s32[8,512,128]{2,1,0:T(8,128)S(1)}, s32[8,512,128]{2,1,0:T(8,128)}, u32[]{:S(2)}) %copy-start) | copy-done | bytes 2097176
  3.5 0.0 copy-start.1
  3.5 0.7 %copy-done.1 = s32[1,1,8,128,1]{3,4,2,1,0:T(1,128)S(1)} copy-done((s32[1,1,8,128,1]{3,4,2,1,0:T(1,128)S(1)}, s32[1,1,8,128,1]{3,4,2,1,0:T(1,128)}, u32[]{:S(2)}) %copy-start.1) | copy-done | bytes 4120
  4.2 0.0 copy-start.2
  4.2 0.7 %copy-done.2 = s32[1,1,8,128]{3,2,1,0:T(8,128)S(1)} copy-done((s32[1,1,8,128]{3,2,1,0:T(8,128)S(1)}, s32[1,1,8,128]{3,2,1,0:T(8,128)}, u32[]{:S(2)}) %copy-start.2) | copy-done | bytes 4120
  4.9 57.1 %shard_map.68 = (f32[2,512,128]{2,1,0:T(8,128)S(1)}, f32[512,128]{1,0:T(8,128)S(1)}) custom-call(bf16[3,8,16,256]{3,2,1,0:T(8,128)(2,1)S(1)} %bitcast.7, s32[8,128]{1,0:T(8,128)S(1)} %bitcast.8, s32[8,128]{1,0:T(8,128)S(1)} %bitcast.9, s32[8,512,128]{2,1,0:T(8,128)S(1)} %copy-done), custom_call_target="tpu_custom_call" | custom-call | tf_op jit(solution)/shard_map/pallas_call | solution.py:290
  61.9 0.8 %copy.12 = f32[2,512,128]{2,1,0:T(8,128)} copy(f32[2,512,128]{2,1,0:T(8,128)S(1)} %get-tuple-element.4) | data formatting | bytes 1048576
  62.7 0.7 %copy.13 = f32[512,128]{1,0:T(8,128)} copy(f32[512,128]{1,0:T(8,128)S(1)} %get-tuple-element.5) | data formatting | bytes 524288
  (1 shorter events, 0.0 us)
Async XLA Ops:
  1.9 1.6 %copy-start = (s32[8,512,128]{2,1,0:T(8,128)S(1)}, s32[8,512,128]{2,1,0:T(8,128)}, u32[]{:S(2)}) copy-start(s32[8,512,128]{2,1,0:T(8,128)} %cells_hbm.1) | copy-start | bytes 6291460
  3.5 0.7 %copy-start.1 = (s32[1,1,8,128,1]{3,4,2,1,0:T(1,128)S(1)}, s32[1,1,8,128,1]{3,4,2,1,0:T(1,128)}, u32[]{:S(2)}) copy-start(s32[1,1,8,128,1]{3,4,2,1,0:T(1,128)} %param.7) | copy-start | bytes 12292
  4.2 0.7 %copy-start.2 = (s32[1,1,8,128]{3,2,1,0:T(8,128)S(1)}, s32[1,1,8,128]{3,2,1,0:T(8,128)}, u32[]{:S(2)}) copy-start(s32[1,1,8,128]{3,2,1,0:T(8,128)} %param.8) | copy-start | bytes 12292
where the time goes:
time: 64.5 us; the launch traced here: 63.4 us
  Pallas kernels  57.1 us (89%)
  local copies, waits for them, and re-layouts  4.67 us (7%)
  other arithmetic  1.05 us (2%)
  between operations  0.66 us (1%)
    pallas_call x1, Pallas kernels, body(): pl.pallas_call(kernel, out_shape=(jax.ShapeDtypeStruct((2, 512, 128), jnp...  57.1 us
    unnamed x8, local copies, waits for them, and re-layouts  4.46 us

commit v1 on v0

--- a/solution.py
+++ b/solution.py
@@ -7,13 +7,15 @@
 
 MESH = pl.DeviceIdType.MESH
 STEPS = 8
-CHUNKS = 2
-PER = STEPS // CHUNKS
 GROUPS = 128
 GROUP_ROWS = 4
 BLOCKS = 16
 WIDTH = 256
 DIMS = ((1, 2, 0), (2, 0, 1), (0, 1, 2))
+PIECES1 = ((0, 2), (2, 6))
+PIECES = ((0, 2), (2, 2), (4, 2), (6, 2))
+NEAR = (1, 3, 2)
+LINE = ((1, 0), (3, 0), (2, 0), (1, 1), (3, 1), (2, 1), (0, 1))
 
 
 def owner_parts(owner):
@@ -24,11 +26,10 @@
     return place[0] * 32 + place[1] * 8 + core * 4 + place[2]
 
 
-def kernel(
-    table_ref, dev_ref, block_ref, cells_hbm, flow_ref, ftle_ref,
-    tab, rep, rcv, cells, pick, sort, ask, asked, first, state, coef,
-    rows_out, rows_in, cols_out, cols_in,
-    cell_sem, own_sem, back_sem, send1, recv1, send2, recv2, send3, recv3, sendq, recvq, sendh, recvh,
+def advect_kernel(
+    base_hbm, grad_hbm, dev_hbm, block_hbm, cells_hbm, state, rows_in, cols_in, rows_out,
+    base, grad, dev_ref, block_ref, cells, tab, rep, rcv, pick, sort, ask, asked, first, coef, cols_out,
+    load_sem, back_sem, send1, recv1, send2, recv2, send3, recv3, sendq, recvq, sendh, recvh,
 ):
     lon = lax.axis_index("lon")
     lat = lax.axis_index("lat")
@@ -47,22 +48,39 @@
     east, west = (lon + 1) % n_lon, (lon + n_lon - 1) % n_lon
     partners = [device(moved(dim, by), (core + flip) % 2) for dim in range(3) for by in (1, 2, 3) for flip in (0, 1)]
     partners += [device(here, 1 - core), (east, lat), (west, lat)]
-
-    cells_copy = pltpu.make_async_copy(cells_hbm, cells, cell_sem)
-    cells_copy.start()
-    own = []
-    for k, (d1, d2, _) in enumerate(DIMS):
-        for c in range(CHUNKS):
-            own.append(
-                pltpu.make_async_copy(
-                    table_ref.at[k, pl.ds(c * PER, PER)], tab.at[k, c, here[d2], here[d1]], own_sem.at[k, c]
-                )
-            )
-            own[-1].start()
-
     barrier = pltpu.get_barrier_semaphore()
     for partner in partners:
         pl.semaphore_signal(barrier, inc=1, device_id=partner, device_id_type=MESH)
+
+    loads = [
+        pltpu.make_async_copy(src, dst, load_sem.at[i])
+        for i, (src, dst) in enumerate(
+            ((base_hbm, base), (grad_hbm, grad), (dev_hbm, dev_ref), (block_hbm, block_ref), (cells_hbm, cells))
+        )
+    ]
+    for load in loads:
+        load.start()
+
+    row = lax.broadcasted_iota(jnp.int32, (256, 256), 0)
+    column = lax.broadcasted_iota(jnp.int32, (256, 256), 1)
+    order = jnp.where(column == (row & 127) * 2 + (row >> 7), 1.0, 0.0).astype(jnp.bfloat16)
+    loads[0].wait()
+    mine = jnp.dot(order, base[...], preferred_element_type=jnp.float32).astype(jnp.bfloat16)
+    for m in range(2):
+        part = mine[m * 128 : (m + 1) * 128].reshape(STEPS, BLOCKS, 128)
+        tab[0, :, here[DIMS[0][1]], here[DIMS[0][0]], :, m * 128 : (m + 1) * 128] = part
+    order = jnp.where(column == (row & 63) * 4 + (row >> 6), 1.0, 0.0).astype(jnp.bfloat16)
+    loads[1].wait()
+    for half in range(2):
+        mine = jnp.dot(
+            order, grad[half * 256 : (half + 1) * 256], preferred_element_type=jnp.float32
+        ).astype(jnp.bfloat16)
+        for m in range(4):
+            k = 1 + m // 2
+            part = mine[m * 64 : (m + 1) * 64].reshape(4, BLOCKS, 128)
+            tab[
+                k, half * 4 : half * 4 + 4, here[DIMS[k][1]], here[DIMS[k][0]], :, m % 2 * 128 : m % 2 * 128 + 128
+            ] = part
     pl.semaphore_wait(barrier, len(partners))
 
     def remote(src, dst, send, recv, target):
@@ -71,35 +89,42 @@
         )
 
     phase1, phase2, phase3, query, back = {}, {}, {}, {}, {}
-    for c in range(CHUNKS):
-        for k, (d1, d2, d3) in enumerate(DIMS):
-            for by in (1, 3, 2):
+    for k, (d1, d2, d3) in enumerate(DIMS):
+        for c, (s0, n) in enumerate(PIECES1):
+            for by in NEAR:
+                ref = tab.at[k, pl.ds(s0, n), here[d2], here[d1]]
                 phase1[k, c, by] = remote(
-                    table_ref.at[k, pl.ds(c * PER, PER)], tab.at[k, c, here[d2], here[d1]],
-                    send1.at[k, c, by - 1], recv1.at[k, c, by - 1], device(moved(d1, by), core),
+                    ref, ref, send1.at[k, c, by - 1], recv1.at[k, c, by - 1], device(moved(d1, by), core)
                 )
+        slot = here[d3] * 2 + core
+        for c, (s0, n) in enumerate(PIECES):
+            for by in NEAR:
+                ref = tab.at[k, pl.ds(s0, n), here[d2]]
                 phase2[k, c, by] = remote(
-                    tab.at[k, c, here[d2]], tab.at[k, c, here[d2]],
-                    send2.at[k, c, by - 1], recv2.at[k, c, by - 1], device(moved(d2, by), core),
+                    ref, ref, send2.at[k, c, by - 1], recv2.at[k, c, by - 1], device(moved(d2, by), core)
                 )
-            mine = here[d3] * 2 + core
-            for i, (by, flip) in enumerate(((1, 0), (3, 0), (2, 0), (1, 1), (3, 1), (2, 1), (0, 1))):
+            for i, (by, flip) in enumerate(LINE):
                 place, which = moved(d3, by), (core + flip) % 2
                 theirs = place[d3] * 2 + which
                 phase3[k, c, i] = remote(
-                    rep.at[k, c, theirs], rcv.at[k, c, mine], send3.at[k, c, i], recv3.at[k, c, i], device(place, which)
+                    rep.at[k, pl.ds(s0, n), theirs], rcv.at[k, pl.ds(s0, n), slot],
+                    send3.at[k, c, i], recv3.at[k, c, i], device(place, which),
                 )
                 if c == 0:
                     query[k, i] = remote(
-                        ask.at[k, theirs // 4], asked.at[k, mine], sendq.at[k, i], recvq.at[k, i], device(place, which)
+                        ask.at[k, theirs // 4], asked.at[k, slot], sendq.at[k, i], recvq.at[k, i], device(place, which)
                     )
-            back[k, c] = pltpu.make_async_copy(rep.at[k, c, mine], rcv.at[k, c, mine], back_sem.at[k, c])
-
-    for c in range(CHUNKS):
-        for by in (1, 3, 2):
+            back[k, c] = pltpu.make_async_copy(
+                rep.at[k, pl.ds(s0, n), slot], rcv.at[k, pl.ds(s0, n), slot], back_sem.at[k, c]
+            )
+
+    for c in range(len(PIECES1)):
+        for by in NEAR:
             for k in range(3):
                 phase1[k, c, by].start()
 
+    loads[2].wait()
+    loads[3].wait()
     lane = lax.broadcasted_iota(jnp.int32, (GROUPS, 128), 1)
     group = lax.broadcasted_iota(jnp.int32, (GROUPS, 128), 0)
     dev_columns = jnp.transpose(dev_ref[...].astype(jnp.float32))
@@ -129,12 +154,15 @@
             query[k, i].start()
         asked[k, here[d3] * 2 + core] = ask[k, here[d3] // 2]
 
-    for c in range(CHUNKS):
-        for k in range(3):
-            own[k * CHUNKS + c].wait()
-            for by in (1, 3, 2):
-                phase1[k, c, by].wait_recv()
-            for by in (1, 3, 2):
+    arrived = 0
+    for c, (s0, n) in enumerate(PIECES):
+        while arrived < len(PIECES1) and PIECES1[arrived][0] < s0 + n:
+            for k in range(3):
+                for by in NEAR:
+                    phase1[k, arrived, by].wait_recv()
+            arrived += 1
+        for by in NEAR:
+            for k in range(3):
                 phase2[k, c, by].start()
 
     dev_int = dev_columns.astype(jnp.int32)
@@ -168,57 +196,46 @@
                 jnp.broadcast_to(rows[:, s : s + 1], (WIDTH, WIDTH)) == block_lane, 1.0, 0.0
             ).astype(jnp.bfloat16)
 
-    for c in range(CHUNKS):
+    for c, (s0, n) in enumerate(PIECES):
         for k in range(3):
-            for by in (1, 3, 2):
+            for by in NEAR:
                 phase2[k, c, by].wait_recv()
-
-            @pl.loop(0, PER)
-            def _(j):
-                found = jnp.dot(
-                    pick[k, c * PER + j], tab[k, c, :, :, j].reshape(WIDTH, WIDTH), preferred_element_type=jnp.float32
-                )
-                rep[k, c, :, j] = found.astype(jnp.bfloat16).reshape(8, 32, WIDTH)
-
+            for s in range(s0, s0 + n):
+                found = jnp.dot(pick[k, s], tab[k, s].reshape(WIDTH, WIDTH), preferred_element_type=jnp.float32)
+                rep[k, s] = found.astype(jnp.bfloat16).reshape(8, 32, WIDTH)
             for i in range(7):
                 phase3[k, c, i].start()
             back[k, c].start()
 
     state[...] = jnp.zeros_like(state)
-    cells_copy.wait()
-    for c in range(CHUNKS):
+    loads[4].wait()
+    for c, (s0, n) in enumerate(PIECES):
         for k in range(3):
             back[k, c].wait()
             for i in range(7):
                 phase3[k, c, i].wait_recv()
 
-        @pl.loop(0, PER)
-        def _(j):
-            step = c * PER + j
+        @pl.loop(s0, s0 + n)
+        def _(step):
             for k in range(3):
-                found = jnp.dot(
-                    sort[k, step], rcv[k, c, :, j].reshape(WIDTH, WIDTH), preferred_element_type=jnp.float32
-                )
+                found = jnp.dot(sort[k, step], rcv[k, step].reshape(WIDTH, WIDTH), preferred_element_type=jnp.float32)
                 coef[2 * k] = found[:, :128]
                 coef[2 * k + 1] = found[:, 128:]
-
-            @pl.loop(0, GROUPS // 8)
-            def _(t):
-                start = pl.multiple_of(t * 8, 8)
-                tables = [coef[m, pl.ds(start, 8), :] for m in range(6)]
+            for start in range(0, GROUPS, 8):
+                tables = [coef[m, start : start + 8, :] for m in range(6)]
                 for q in range(GROUP_ROWS):
-                    index = cells[step, pl.ds(t * 32 + q, 8, stride=GROUP_ROWS), :]
+                    index = cells[step, pl.ds(start * GROUP_ROWS + q, 8, stride=GROUP_ROWS), :]
                     vx, vy, gxx, gxy, gyx, gyy = (
                         jnp.take_along_axis(table, index, axis=1, mode="promise_in_bounds") for table in tables
                     )
-                    px, py = state[0, q, pl.ds(start, 8), :], state[1, q, pl.ds(start, 8), :]
+                    px, py = state[0, q, start : start + 8, :], state[1, q, start : start + 8, :]
                     kx = vx + (gxx * px + gxy * py)
                     ky = vy + (gyx * px + gyy * py)
                     wx, wy = kx, ky
                     for part in (0.25, 1.0 / 3.0, 0.5):
                         wx, wy = kx + part * (gxx * wx + gxy * wy), ky + part * (gyx * wx + gyy * wy)
-                    state[0, q, pl.ds(start, 8), :] = px + wx
-                    state[1, q, pl.ds(start, 8), :] = py + wy
+                    state[0, q, start : start + 8, :] = px + wx
+                    state[1, q, start : start + 8, :] = py + wy
 
     rows_out[...] = jnp.zeros_like(rows_out)
     cols_out[...] = jnp.zeros_like(cols_out)
@@ -237,11 +254,23 @@
     for i, lon_to in enumerate((east, west)):
         halo.append(remote(cols_out, cols_in.at[i], sendh.at[2 + i], recvh.at[2 + i], (lon_to, lat)))
         halo[-1].start()
+    for copies in (phase1, phase2, phase3, query):
+        for copy in copies.values():
+            copy.wait_send()
+    for copy in halo:
+        copy.wait_send()
+        copy.wait_recv()
+
+
+def stretch_kernel(state, rows_in, cols_in, rows_out, flow_hbm, ftle_hbm, flow, ftle, sem):
+    lat = lax.axis_index("lat")
     for comp in range(2):
         for q in range(GROUP_ROWS):
-            flow_ref[comp, pl.ds(q, GROUPS, stride=GROUP_ROWS), :] = state[comp, q]
-    for copy in halo:
-        copy.wait_recv()
+            flow[comp, pl.ds(q, GROUPS, stride=GROUP_ROWS), :] = state[comp, q]
+    flow_copy = pltpu.make_async_copy(flow, flow_hbm, sem.at[0])
+    flow_copy.start()
+    lane = lax.broadcasted_iota(jnp.int32, (GROUPS, 128), 1)
+    group = lax.broadcasted_iota(jnp.int32, (GROUPS, 128), 0)
     south_own, north_own = lat == 0, lat == 3
     at_west, at_east = lane == 0, lane == 127
     bottom, top = group == 0, group == GROUPS - 1
@@ -273,55 +302,65 @@
         green_xy = map_xx * map_xy + map_yx * map_yy
         half_diff = 0.5 * (green_xx - green_yy)
         largest = 0.5 * (green_xx + green_yy) + jnp.sqrt(half_diff * half_diff + green_xy * green_xy)
-        ftle_ref[pl.ds(q, GROUPS, stride=GROUP_ROWS), :] = 0.5 * jnp.log(largest)
-
-    for copies in (phase1, phase2, phase3, query):
-        for copy in copies.values():
-            copy.wait_send()
-    for copy in halo:
-        copy.wait_send()
+        ftle[pl.ds(q, GROUPS, stride=GROUP_ROWS), :] = 0.5 * jnp.log(largest)
+    ftle_copy = pltpu.make_async_copy(ftle, ftle_hbm, sem.at[1])
+    ftle_copy.start()
+    flow_copy.wait()
+    ftle_copy.wait()
 
 
 def body(vel_base, vel_grad, route_dev, route_block, seed_cells):
-    table = jnp.concatenate([vel_base[0, 0], vel_grad[0, 0]], axis=2).reshape(STEPS, BLOCKS, 3, WIDTH)
-    table = jnp.transpose(table, (2, 0, 1, 3))
     dma = pltpu.SemaphoreType.DMA
     vmem = pl.BlockSpec(memory_space=pltpu.VMEM)
-    return pl.pallas_call(
-        kernel,
+    hbm = pl.BlockSpec(memory_space=pltpu.HBM)
+    bf16, f32, i32 = jnp.bfloat16, jnp.float32, jnp.int32
+    moved = pl.pallas_call(
+        advect_kernel,
         out_shape=(
-            jax.ShapeDtypeStruct((2, 512, 128), jnp.float32),
-            jax.ShapeDtypeStruct((512, 128), jnp.float32),
+            jax.ShapeDtypeStruct((2, GROUP_ROWS, GROUPS, 128), f32),
+            jax.ShapeDtypeStruct((2, 8, 128), f32),
+            jax.ShapeDtypeStruct((2, GROUP_ROWS, 8, 128), f32),
+            jax.ShapeDtypeStruct((8, 128), f32),
         ),
-        in_specs=[vmem, vmem, vmem, pl.BlockSpec(memory_space=pl.ANY)],
-        out_specs=(vmem, vmem),
+        in_specs=[hbm] * 5,
+        out_specs=(vmem,) * 4,
         scratch_shapes=[
-            pltpu.VMEM((3, CHUNKS, 4, 4, PER, BLOCKS, WIDTH), jnp.bfloat16),
-            pltpu.VMEM((3, CHUNKS, 8, PER, 32, WIDTH), jnp.bfloat16),
-            pltpu.VMEM((3, CHUNKS, 8, PER, 32, WIDTH), jnp.bfloat16),
-            pltpu.VMEM((STEPS, 512, 128), jnp.int32),
-            pltpu.VMEM((3, STEPS, WIDTH, WIDTH), jnp.bfloat16),
-            pltpu.VMEM((3, STEPS, GROUPS, WIDTH), jnp.bfloat16),
-            pltpu.VMEM((3, 2, 8, 128), jnp.float32),
-            pltpu.VMEM((3, 8, 8, 128), jnp.float32),
-            pltpu.VMEM((2, STEPS, 128), jnp.float32),
-            pltpu.VMEM((2, GROUP_ROWS, GROUPS, 128), jnp.float32),
-            pltpu.VMEM((6, GROUPS, 128), jnp.float32),
-            pltpu.VMEM((8, 128), jnp.float32),
-            pltpu.VMEM((2, 8, 128), jnp.float32),
-            pltpu.VMEM((GROUP_ROWS, 8, 128), jnp.float32),
-            pltpu.VMEM((2, GROUP_ROWS, 8, 128), jnp.float32),
-            dma, dma((3, CHUNKS)), dma((3, CHUNKS)),
-            dma((3, CHUNKS, 3)), dma((3, CHUNKS, 3)),
-            dma((3, CHUNKS, 3)), dma((3, CHUNKS, 3)),
-            dma((3, CHUNKS, 7)), dma((3, CHUNKS, 7)),
+            pltpu.VMEM((256, 128), bf16),
+            pltpu.VMEM((512, 128), bf16),
+            pltpu.VMEM((STEPS, GROUPS), i32),
+            pltpu.VMEM((STEPS, GROUPS), i32),
+            pltpu.VMEM((STEPS, 512, 128), i32),
+            pltpu.VMEM((3, STEPS, 4, 4, BLOCKS, WIDTH), bf16),
+            pltpu.VMEM((3, STEPS, 8, 32, WIDTH), bf16),
+            pltpu.VMEM((3, STEPS, 8, 32, WIDTH), bf16),
+            pltpu.VMEM((3, STEPS, WIDTH, WIDTH), bf16),
+            pltpu.VMEM((3, STEPS, GROUPS, WIDTH), bf16),
+            pltpu.VMEM((3, 2, 8, 128), f32),
+            pltpu.VMEM((3, 8, 8, 128), f32),
+            pltpu.VMEM((2, STEPS, 128), f32),
+            pltpu.VMEM((6, GROUPS, 128), f32),
+            pltpu.VMEM((GROUP_ROWS, 8, 128), f32),
+            dma((5,)), dma((3, len(PIECES))),
+            dma((3, len(PIECES1), 3)), dma((3, len(PIECES1), 3)),
+            dma((3, len(PIECES), 3)), dma((3, len(PIECES), 3)),
+            dma((3, len(PIECES), 7)), dma((3, len(PIECES), 7)),
             dma((3, 7)), dma((3, 7)),
             dma((4,)), dma((4,)),
         ],
-        compiler_params=pltpu.CompilerParams(
-            collective_id=0, has_side_effects=True, vmem_limit_bytes=48 << 20
-        ),
-    )(table, route_dev[0, 0, :, :, 0], route_block[0, 0], seed_cells)
+        compiler_params=pltpu.CompilerParams(collective_id=0, has_side_effects=True, vmem_limit_bytes=48 << 20),
+    )(
+        *(pltpu.with_memory_space_constraint(a, pltpu.HBM) for a in (
+        vel_base.reshape(256, 128), vel_grad.reshape(512, 128), route_dev.reshape(STEPS, GROUPS),
+        route_block.reshape(STEPS, GROUPS), seed_cells)),
+    )
+    return pl.pallas_call(
+        stretch_kernel,
+        out_shape=(jax.ShapeDtypeStruct((2, 512, 128), f32), jax.ShapeDtypeStruct((512, 128), f32)),
+        in_specs=[vmem] * 4,
+        out_specs=(hbm, hbm),
+        scratch_shapes=[pltpu.VMEM((2, 512, 128), f32), pltpu.VMEM((512, 128), f32), dma((2,))],
+        compiler_params=pltpu.CompilerParams(vmem_limit_bytes=6 << 20),
+    )(*moved)
 
 
 def solution(mesh):

time: 64.5 us -> 47.5 us (0.74); the launches traced: 63.4 us -> 47.4 us
  Pallas kernels: 57.1 us -> 46.8 us
  local copies, waits for them, and re-layouts: 4.67 us -> 0 us
  other arithmetic: 1.05 us -> 0 us
    pallas_call x1 -> x2, Pallas kernels: 57.1 us -> 46.8 us  [the longest x1 44.9 us: body(): pl.pallas_call(advect_kernel, out_shape=(jax.ShapeDtypeStruct((2, GROUP_R...]
    unnamed x8 -> x0, local copies, waits for them, and re-layouts: 4.46 us -> none
    concatenate x1 -> x0, other arithmetic: 1.05 us -> none  [body(): jnp.concatenate([vel_base[0, 0], vel_grad[0, 0]], axis=2)]
where the time goes in v1:
time: 47.5 us; the launch traced here: 47.4 us
  Pallas kernels  46.8 us (99%)
  between operations  0.64 us (1%)
    pallas_call x1, Pallas kernels, body(): pl.pallas_call(advect_kernel, out_shape=(jax.ShapeDtypeStruct((2, GROUP_R...  44.9 us
    pallas_call x1, Pallas kernels, body(): pl.pallas_call(stretch_kernel, out_shape=(jax.ShapeDtypeStruct((2, 512, 1...  1.89 us

profile of v1, /device:TPU:1, one launch (start us, length us, event | category | flops | bytes accessed | tf_op | source)
XLA Modules:
  0.0 47.4 jit_solution(8391234147801237798)
XLA Ops:
  0.6 44.9 %shard_map.68 = (f32[2,4,128,128]{3,2,1,0:T(8,128)S(1)}, f32[2,8,128]{2,1,0:T(8,128)S(1)}, f32[2,4,8,128]{3,2,1,0:T(8,128)S(1)}, f32[8,128]{1,0:T(8,128)S(1)}) custom-call(bf16[256,128]{1,0:T(8,128)(2,1)} %bitcast.5, bf16[512,128]{1,0:T(8,128)(2,1)} %bitcast.4, s32[8,128]{1,0:T(8,128)} %bitcast.6, s32[8,128]{1,0:T(8,128)} %bitcast.7, s32[8,512,128]{2,1,0:T(8,128)} %cells_hbm.1), custom_call_target="tpu_custom_call" | custom-call | tf_op jit(solution)/shard_map/pallas_call | solution.py:317
  45.5 1.9 %shard_map.69 = (f32[2,512,128]{2,1,0:T(8,128)}, f32[512,128]{1,0:T(8,128)}) custom-call(f32[2,4,128,128]{3,2,1,0:T(8,128)S(1)} %get-tuple-element.6.state, f32[2,8,128]{2,1,0:T(8,128)S(1)} %get-tuple-element.7.rows_in, f32[2,4,8,128]{3,2,1,0:T(8,128)S(1)} %get-tuple-element.8.cols_in, f32[8,128]{1,0:T(8,128)S(1)} %get-tuple-element.9.rows_out), custom_call_target="tpu_custom_call" | custom-call | tf_op jit(solution)/shard_map/pallas_call | solution.py:356

commit v2 on v1

--- a/solution.py
+++ b/solution.py
@@ -28,7 +28,7 @@
 
 def advect_kernel(
     base_hbm, grad_hbm, dev_hbm, block_hbm, cells_hbm, state, rows_in, cols_in, rows_out,
-    base, grad, dev_ref, block_ref, cells, tab, rep, rcv, pick, sort, ask, asked, first, coef, cols_out,
+    base, grad, dev_ref, block_ref, cells, tab, rep, rcv, pick, sort, ask, asked, first, coef, edge_cells, edge, cols_out,
     load_sem, back_sem, send1, recv1, send2, recv2, send3, recv3, sendq, recvq, sendh, recvh,
 ):
     lon = lax.axis_index("lon")
@@ -68,7 +68,7 @@
     mine = jnp.dot(order, base[...], preferred_element_type=jnp.float32).astype(jnp.bfloat16)
     for m in range(2):
         part = mine[m * 128 : (m + 1) * 128].reshape(STEPS, BLOCKS, 128)
-        tab[0, :, here[DIMS[0][1]], here[DIMS[0][0]], :, m * 128 : (m + 1) * 128] = part
+        tab[0, :, 0, 0, :, m * 128 : (m + 1) * 128] = part
     order = jnp.where(column == (row & 63) * 4 + (row >> 6), 1.0, 0.0).astype(jnp.bfloat16)
     loads[1].wait()
     for half in range(2):
@@ -78,9 +78,7 @@
         for m in range(4):
             k = 1 + m // 2
             part = mine[m * 64 : (m + 1) * 64].reshape(4, BLOCKS, 128)
-            tab[
-                k, half * 4 : half * 4 + 4, here[DIMS[k][1]], here[DIMS[k][0]], :, m % 2 * 128 : m % 2 * 128 + 128
-            ] = part
+            tab[k, half * 4 : half * 4 + 4, 0, 0, :, m % 2 * 128 : m % 2 * 128 + 128] = part
     pl.semaphore_wait(barrier, len(partners))
 
     def remote(src, dst, send, recv, target):
@@ -88,20 +86,25 @@
             src_ref=src, dst_ref=dst, send_sem=send, recv_sem=recv, device_id=target, device_id_type=MESH
         )
 
-    phase1, phase2, phase3, query, back = {}, {}, {}, {}, {}
+    phase1, early, phase2, phase3, query, back = {}, {}, {}, {}, {}, {}
     for k, (d1, d2, d3) in enumerate(DIMS):
         for c, (s0, n) in enumerate(PIECES1):
+            steps = pl.ds(s0, n)
             for by in NEAR:
-                ref = tab.at[k, pl.ds(s0, n), here[d2], here[d1]]
                 phase1[k, c, by] = remote(
-                    ref, ref, send1.at[k, c, by - 1], recv1.at[k, c, by - 1], device(moved(d1, by), core)
+                    tab.at[k, steps, 0, 0], tab.at[k, steps, 0, by],
+                    send1.at[k, c, by - 1], recv1.at[k, c, by - 1], device(moved(d1, by), core),
+                )
+                early[k, c, by] = remote(
+                    tab.at[k, steps, 0, 0], tab.at[k, steps, by, 0],
+                    send1.at[k, c, by + 2], recv1.at[k, c, by + 2], device(moved(d2, by), core),
                 )
         slot = here[d3] * 2 + core
         for c, (s0, n) in enumerate(PIECES):
             for by in NEAR:
-                ref = tab.at[k, pl.ds(s0, n), here[d2]]
                 phase2[k, c, by] = remote(
-                    ref, ref, send2.at[k, c, by - 1], recv2.at[k, c, by - 1], device(moved(d2, by), core)
+                    tab.at[k, pl.ds(s0, n), 0, pl.ds(1, 3)], tab.at[k, pl.ds(s0, n), by, pl.ds(1, 3)],
+                    send2.at[k, c, by - 1], recv2.at[k, c, by - 1], device(moved(d2, by), core),
                 )
             for i, (by, flip) in enumerate(LINE):
                 place, which = moved(d3, by), (core + flip) % 2
@@ -118,10 +121,11 @@
                 rep.at[k, pl.ds(s0, n), slot], rcv.at[k, pl.ds(s0, n), slot], back_sem.at[k, c]
             )
 
-    for c in range(len(PIECES1)):
-        for by in NEAR:
-            for k in range(3):
-                phase1[k, c, by].start()
+    for copies in (phase1, early):
+        for c in range(len(PIECES1)):
+            for by in NEAR:
+                for k in range(3):
+                    copies[k, c, by].start()
 
     loads[2].wait()
     loads[3].wait()
@@ -149,7 +153,8 @@
                 jnp.take_along_axis(first[0], index, axis=1, mode="promise_in_bounds"),
                 jnp.take_along_axis(first[1], index, axis=1, mode="promise_in_bounds"),
             )
-            ask[k, half] = chosen + (((number >> 1) & 15) * BLOCKS).astype(jnp.float32)
+            back_by = (((here[d2] - place[d2]) & 3) * 4 + ((here[d1] - place[d1]) & 3)) * BLOCKS
+            ask[k, half] = chosen + back_by.astype(jnp.float32)
         for i in range(7):
             query[k, i].start()
         asked[k, here[d3] * 2 + core] = ask[k, here[d3] // 2]
@@ -177,6 +182,19 @@
         for k, (d1, d2, d3) in enumerate(DIMS):
             slot = (((place[d3] * 2 + which) * 4 + place[d2]) * 4 + place[d1]) * 2 + rank
             sort[k, s] = jnp.where(jnp.broadcast_to(slot, (GROUPS, WIDTH)) == slot_lane, -1.0 / STEPS, 0.0).astype(jnp.bfloat16)
+
+    loads[4].wait()
+
+    @pl.loop(0, STEPS)
+    def _(step):
+        packed = pltpu.roll(cells[step, pl.ds(0, GROUPS, stride=GROUP_ROWS), :], 1, 1)
+        for q in range(1, GROUP_ROWS):
+            turned = pltpu.roll(cells[step, pl.ds(q, GROUPS, stride=GROUP_ROWS), :], 2 * q + 1, 1)
+            packed = jnp.where(lane // 2 == q, turned, packed)
+        edge_cells[step] = packed
+
+    state[...] = jnp.zeros_like(state)
+    edge[...] = jnp.zeros_like(edge)
 
     block_lane = lax.broadcasted_iota(jnp.int32, (WIDTH, WIDTH), 1).astype(jnp.float32)
     for k, (_, _, d3) in enumerate(DIMS):
@@ -196,7 +214,13 @@
                 jnp.broadcast_to(rows[:, s : s + 1], (WIDTH, WIDTH)) == block_lane, 1.0, 0.0
             ).astype(jnp.bfloat16)
 
+    arrived = 0
     for c, (s0, n) in enumerate(PIECES):
+        while arrived < len(PIECES1) and PIECES1[arrived][0] < s0 + n:
+            for k in range(3):
+                for by in NEAR:
+                    early[k, arrived, by].wait_recv()
+            arrived += 1
         for k in range(3):
             for by in NEAR:
                 phase2[k, c, by].wait_recv()
@@ -207,54 +231,81 @@
                 phase3[k, c, i].start()
             back[k, c].start()
 
-    state[...] = jnp.zeros_like(state)
-    loads[4].wait()
-    for c, (s0, n) in enumerate(PIECES):
+    def collect(c):
         for k in range(3):
             back[k, c].wait()
             for i in range(7):
                 phase3[k, c, i].wait_recv()
 
+    def sort_blocks(step, at):
+        for k in range(3):
+            found = jnp.dot(sort[k, step], rcv[k, step].reshape(WIDTH, WIDTH), preferred_element_type=jnp.float32)
+            coef[at, 2 * k] = found[:, :128]
+            coef[at, 2 * k + 1] = found[:, 128:]
+
+    def advance(at, start, index, px, py):
+        vx, vy, gxx, gxy, gyx, gyy = (
+            jnp.take_along_axis(coef[at, m, start : start + 8, :], index, axis=1, mode="promise_in_bounds")
+            for m in range(6)
+        )
+        kx = vx + (gxx * px + gxy * py)
+        ky = vy + (gyx * px + gyy * py)
+        wx, wy = kx, ky
+        for part in (0.25, 1.0 / 3.0, 0.5):
+            wx, wy = kx + part * (gxx * wx + gxy * wy), ky + part * (gyx * wx + gyy * wy)
+        return px + wx, py + wy
+
+    def advance_edge(start, steps):
+        rows = slice(start, start + 8)
+        px, py = edge[0, rows, :], edge[1, rows, :]
+        for at, step in steps:
+            px, py = advance(at, start, edge_cells[step, rows, :], px, py)
+        edge[0, rows, :], edge[1, rows, :] = px, py
+
+    def advance_rows(start, steps):
+        rows = slice(start, start + 8)
+        for q in range(GROUP_ROWS):
+            px, py = state[0, q, rows, :], state[1, q, rows, :]
+            for at, step in steps:
+                index = cells[step, pl.ds(start * GROUP_ROWS + q, 8, stride=GROUP_ROWS), :]
+                px, py = advance(at, start, index, px, py)
+            state[0, q, rows, :], state[1, q, rows, :] = px, py
+
+    for c, (s0, n) in enumerate(PIECES[:-1]):
+        collect(c)
+
         @pl.loop(s0, s0 + n)
         def _(step):
-            for k in range(3):
-                found = jnp.dot(sort[k, step], rcv[k, step].reshape(WIDTH, WIDTH), preferred_element_type=jnp.float32)
-                coef[2 * k] = found[:, :128]
-                coef[2 * k + 1] = found[:, 128:]
+            sort_blocks(step, 0)
             for start in range(0, GROUPS, 8):
-                tables = [coef[m, start : start + 8, :] for m in range(6)]
-                for q in range(GROUP_ROWS):
-                    index = cells[step, pl.ds(start * GROUP_ROWS + q, 8, stride=GROUP_ROWS), :]
-                    vx, vy, gxx, gxy, gyx, gyy = (
-                        jnp.take_along_axis(table, index, axis=1, mode="promise_in_bounds") for table in tables
-                    )
-                    px, py = state[0, q, start : start + 8, :], state[1, q, start : start + 8, :]
-                    kx = vx + (gxx * px + gxy * py)
-                    ky = vy + (gyx * px + gyy * py)
-                    wx, wy = kx, ky
-                    for part in (0.25, 1.0 / 3.0, 0.5):
-                        wx, wy = kx + part * (gxx * wx + gxy * wy), ky + part * (gyx * wx + gyy * wy)
-                    state[0, q, start : start + 8, :] = px + wx
-                    state[1, q, start : start + 8, :] = py + wy
-
+                advance_edge(start, [(0, step)])
+                advance_rows(start, [(0, step)])
+
+    s0, n = PIECES[-1]
+    collect(len(PIECES) - 1)
+    steps = [(i, s0 + i) for i in range(n)]
+    for at, step in steps:
+        sort_blocks(step, at)
+    for start in range(0, GROUPS, 8):
+        advance_edge(start, steps)
+    for comp in range(2):
+        cols_out[comp] = jnp.transpose(edge[comp])[:8, :]
+    halo = []
+    for i, lon_to in enumerate((east, west)):
+        halo.append(remote(cols_out, cols_in.at[i], sendh.at[i], recvh.at[i], (lon_to, lat)))
+        halo[-1].start()
+    for start in (0, GROUPS - 8):
+        advance_rows(start, steps)
     rows_out[...] = jnp.zeros_like(rows_out)
-    cols_out[...] = jnp.zeros_like(cols_out)
     for comp in range(2):
         rows_out[comp : comp + 1, :] = state[comp, 0, 0:1, :]
         rows_out[2 + comp : 3 + comp, :] = state[comp, GROUP_ROWS - 1, GROUPS - 1 : GROUPS, :]
-    halo = []
     for i, by in enumerate((1, 3)):
-        halo.append(remote(rows_out, rows_in.at[i], sendh.at[i], recvh.at[i], device(moved(2, by), core)))
+        halo.append(remote(rows_out, rows_in.at[i], sendh.at[2 + i], recvh.at[2 + i], device(moved(2, by), core)))
         halo[-1].start()
-    for comp in range(2):
-        for q in range(GROUP_ROWS):
-            turned = jnp.transpose(state[comp, q])
-            cols_out[q, comp : comp + 1, :] = turned[0:1, :]
-            cols_out[q, 2 + comp : 3 + comp, :] = turned[127:128, :]
-    for i, lon_to in enumerate((east, west)):
-        halo.append(remote(cols_out, cols_in.at[i], sendh.at[2 + i], recvh.at[2 + i], (lon_to, lat)))
-        halo[-1].start()
-    for copies in (phase1, phase2, phase3, query):
+    for start in range(8, GROUPS - 8, 8):
+        advance_rows(start, steps)
+    for copies in (phase1, early, phase2, phase3, query):
         for copy in copies.values():
             copy.wait_send()
     for copy in halo:
@@ -278,10 +329,11 @@
     for comp in range(2):
         south = jnp.where(south_own, rows_out[comp : comp + 1, :], rows_in[0, 2 + comp : 3 + comp, :])
         north = jnp.where(north_own, rows_out[2 + comp : 3 + comp, :], rows_in[1, comp : comp + 1, :])
+        from_west, from_east = jnp.transpose(cols_in[0, comp]), jnp.transpose(cols_in[1, comp])
         for q in range(GROUP_ROWS):
             own_rows = state[comp, q]
-            west_column = jnp.transpose(cols_in[0, q])[:, 2 + comp : 3 + comp]
-            east_column = jnp.transpose(cols_in[1, q])[:, comp : comp + 1]
+            west_column = from_west[:, 2 * q : 2 * q + 1]
+            east_column = from_east[:, 2 * q + 1 : 2 * q + 2]
             low = jnp.where(at_west, west_column, pltpu.roll(own_rows, 1, 1))
             high = jnp.where(at_east, east_column, pltpu.roll(own_rows, 127, 1))
             diffs[comp, q, 0] = (high - low) * 0.5
@@ -319,7 +371,7 @@
         out_shape=(
             jax.ShapeDtypeStruct((2, GROUP_ROWS, GROUPS, 128), f32),
             jax.ShapeDtypeStruct((2, 8, 128), f32),
-            jax.ShapeDtypeStruct((2, GROUP_ROWS, 8, 128), f32),
+            jax.ShapeDtypeStruct((2, 2, 8, 128), f32),
             jax.ShapeDtypeStruct((8, 128), f32),
         ),
         in_specs=[hbm] * 5,
@@ -338,10 +390,12 @@
             pltpu.VMEM((3, 2, 8, 128), f32),
             pltpu.VMEM((3, 8, 8, 128), f32),
             pltpu.VMEM((2, STEPS, 128), f32),
-            pltpu.VMEM((6, GROUPS, 128), f32),
-            pltpu.VMEM((GROUP_ROWS, 8, 128), f32),
+            pltpu.VMEM((PIECES[-1][1], 6, GROUPS, 128), f32),
+            pltpu.VMEM((STEPS, GROUPS, 128), i32),
+            pltpu.VMEM((2, GROUPS, 128), f32),
+            pltpu.VMEM((2, 8, 128), f32),
             dma((5,)), dma((3, len(PIECES))),
-            dma((3, len(PIECES1), 3)), dma((3, len(PIECES1), 3)),
+            dma((3, len(PIECES1), 6)), dma((3, len(PIECES1), 6)),
             dma((3, len(PIECES), 3)), dma((3, len(PIECES), 3)),
             dma((3, len(PIECES), 7)), dma((3, len(PIECES), 7)),
             dma((3, 7)), dma((3, 7)),

time: 47.5 us -> 45.9 us (0.966)
  Pallas kernels: 46.8 us -> 45 us
    pallas_call x1, Pallas kernels: 44.9 us -> 43.2 us  [body(): pl.pallas_call(advect_kernel, out_shape=(jax.ShapeDtypeStruct((2, GROUP_R...]
where the time goes in v2:
time: 45.9 us; the launch traced here: 45.8 us
  Pallas kernels  45 us (98%)
  between operations  0.8 us (2%)
    pallas_call x1, Pallas kernels, body(): pl.pallas_call(advect_kernel, out_shape=(jax.ShapeDtypeStruct((2, GROUP_R...  43.2 us
    pallas_call x1, Pallas kernels, body(): pl.pallas_call(stretch_kernel, out_shape=(jax.ShapeDtypeStruct((2, 512, 1...  1.77 us

profile of v2, /device:TPU:1, one launch (start us, length us, event | category | flops | bytes accessed | tf_op | source)
XLA Modules:
  0.0 45.8 jit_solution(5046965591528358079)
XLA Ops:
  0.6 43.2 %shard_map.68 = (f32[2,4,128,128]{3,2,1,0:T(8,128)S(1)}, f32[2,8,128]{2,1,0:T(8,128)S(1)}, f32[2,2,8,128]{3,2,1,0:T(8,128)S(1)}, f32[8,128]{1,0:T(8,128)S(1)}) custom-call(bf16[256,128]{1,0:T(8,128)(2,1)} %bitcast.5, bf16[512,128]{1,0:T(8,128)(2,1)} %bitcast.4, s32[8,128]{1,0:T(8,128)} %bitcast.6, s32[8,128]{1,0:T(8,128)} %bitcast.7, s32[8,512,128]{2,1,0:T(8,128)} %cells_hbm.1), custom_call_target="tpu_custom_call" | custom-call | tf_op jit(solution)/shard_map/pallas_call | solution.py:369
  43.9 1.8 %shard_map.69 = (f32[2,512,128]{2,1,0:T(8,128)}, f32[512,128]{1,0:T(8,128)}) custom-call(f32[2,4,128,128]{3,2,1,0:T(8,128)S(1)} %get-tuple-element.6.state, f32[2,8,128]{2,1,0:T(8,128)S(1)} %get-tuple-element.7.rows_in, f32[2,2,8,128]{3,2,1,0:T(8,128)S(1)} %get-tuple-element.8.cols_in, f32[8,128]{1,0:T(8,128)S(1)} %get-tuple-element.9.rows_out), custom_call_target="tpu_custom_call" | custom-call | tf_op jit(solution)/shard_map/pallas_call | solution.py:410

commit v3 on v2

--- a/solution.py
+++ b/solution.py
@@ -12,8 +12,9 @@
 BLOCKS = 16
 WIDTH = 256
 DIMS = ((1, 2, 0), (2, 0, 1), (0, 1, 2))
-PIECES1 = ((0, 2), (2, 6))
-PIECES = ((0, 2), (2, 2), (4, 2), (6, 2))
+PIECES1 = ((0, 8),)
+PIECES2 = ((0, 4), (4, 4))
+PIECES = ((0, 4), (4, 4))
 NEAR = (1, 3, 2)
 LINE = ((1, 0), (3, 0), (2, 0), (1, 1), (3, 1), (2, 1), (0, 1))
 
@@ -100,17 +101,18 @@
                     send1.at[k, c, by + 2], recv1.at[k, c, by + 2], device(moved(d2, by), core),
                 )
         slot = here[d3] * 2 + core
-        for c, (s0, n) in enumerate(PIECES):
+        for c, (s0, n) in enumerate(PIECES2):
             for by in NEAR:
                 phase2[k, c, by] = remote(
                     tab.at[k, pl.ds(s0, n), 0, pl.ds(1, 3)], tab.at[k, pl.ds(s0, n), by, pl.ds(1, 3)],
                     send2.at[k, c, by - 1], recv2.at[k, c, by - 1], device(moved(d2, by), core),
                 )
+        for c, (s0, n) in enumerate(PIECES):
             for i, (by, flip) in enumerate(LINE):
                 place, which = moved(d3, by), (core + flip) % 2
                 theirs = place[d3] * 2 + which
                 phase3[k, c, i] = remote(
-                    rep.at[k, pl.ds(s0, n), theirs], rcv.at[k, pl.ds(s0, n), slot],
+                    rep.at[k, theirs, pl.ds(s0, n)], rcv.at[k, slot, pl.ds(s0, n)],
                     send3.at[k, c, i], recv3.at[k, c, i], device(place, which),
                 )
                 if c == 0:
@@ -118,7 +120,7 @@
                         ask.at[k, theirs // 4], asked.at[k, slot], sendq.at[k, i], recvq.at[k, i], device(place, which)
                     )
             back[k, c] = pltpu.make_async_copy(
-                rep.at[k, pl.ds(s0, n), slot], rcv.at[k, pl.ds(s0, n), slot], back_sem.at[k, c]
+                rep.at[k, slot, pl.ds(s0, n)], rcv.at[k, slot, pl.ds(s0, n)], back_sem.at[k, c]
             )
 
     for copies in (phase1, early):
@@ -160,7 +162,7 @@
         asked[k, here[d3] * 2 + core] = ask[k, here[d3] // 2]
 
     arrived = 0
-    for c, (s0, n) in enumerate(PIECES):
+    for c, (s0, n) in enumerate(PIECES2):
         while arrived < len(PIECES1) and PIECES1[arrived][0] < s0 + n:
             for k in range(3):
                 for by in NEAR:
@@ -214,8 +216,8 @@
                 jnp.broadcast_to(rows[:, s : s + 1], (WIDTH, WIDTH)) == block_lane, 1.0, 0.0
             ).astype(jnp.bfloat16)
 
-    arrived = 0
-    for c, (s0, n) in enumerate(PIECES):
+    arrived = sent = 0
+    for c, (s0, n) in enumerate(PIECES2):
         while arrived < len(PIECES1) and PIECES1[arrived][0] < s0 + n:
             for k in range(3):
                 for by in NEAR:
@@ -224,12 +226,15 @@
         for k in range(3):
             for by in NEAR:
                 phase2[k, c, by].wait_recv()
-            for s in range(s0, s0 + n):
-                found = jnp.dot(pick[k, s], tab[k, s].reshape(WIDTH, WIDTH), preferred_element_type=jnp.float32)
-                rep[k, s] = found.astype(jnp.bfloat16).reshape(8, 32, WIDTH)
-            for i in range(7):
-                phase3[k, c, i].start()
-            back[k, c].start()
+        while sent < len(PIECES) and sum(PIECES[sent]) <= s0 + n:
+            for k in range(3):
+                for s in range(PIECES[sent][0], sum(PIECES[sent])):
+                    found = jnp.dot(pick[k, s], tab[k, s].reshape(WIDTH, WIDTH), preferred_element_type=jnp.float32)
+                    rep[k, :, s] = found.astype(jnp.bfloat16).reshape(8, 32, WIDTH)
+                for i in range(7):
+                    phase3[k, sent, i].start()
+                back[k, sent].start()
+            sent += 1
 
     def collect(c):
         for k in range(3):
@@ -239,7 +244,7 @@
 
     def sort_blocks(step, at):
         for k in range(3):
-            found = jnp.dot(sort[k, step], rcv[k, step].reshape(WIDTH, WIDTH), preferred_element_type=jnp.float32)
+            found = jnp.dot(sort[k, step], rcv[k, :, step].reshape(WIDTH, WIDTH), preferred_element_type=jnp.float32)
             coef[at, 2 * k] = found[:, :128]
             coef[at, 2 * k + 1] = found[:, 128:]
 
@@ -396,7 +401,7 @@
             pltpu.VMEM((2, 8, 128), f32),
             dma((5,)), dma((3, len(PIECES))),
             dma((3, len(PIECES1), 6)), dma((3, len(PIECES1), 6)),
-            dma((3, len(PIECES), 3)), dma((3, len(PIECES), 3)),
+            dma((3, len(PIECES2), 3)), dma((3, len(PIECES2), 3)),
             dma((3, len(PIECES), 7)), dma((3, len(PIECES), 7)),
             dma((3, 7)), dma((3, 7)),
             dma((4,)), dma((4,)),

time: 45.9 us -> 44.9 us (0.978)
  Pallas kernels: 45 us -> 44.1 us
    pallas_call x1, Pallas kernels: 43.2 us -> 42.4 us  [body(): pl.pallas_call(advect_kernel, out_shape=(jax.ShapeDtypeStruct((2, GROUP_R...]
where the time goes in v3:
time: 44.9 us; the launch traced here: 44.8 us
  Pallas kernels  44.1 us (98%)
  between operations  0.64 us (1%)
    pallas_call x1, Pallas kernels, body(): pl.pallas_call(advect_kernel, out_shape=(jax.ShapeDtypeStruct((2, GROUP_R...  42.4 us
    pallas_call x1, Pallas kernels, body(): pl.pallas_call(stretch_kernel, out_shape=(jax.ShapeDtypeStruct((2, 512, 1...  1.77 us

profile of v3, /device:TPU:1, one launch (start us, length us, event | category | flops | bytes accessed | tf_op | source)
XLA Modules:
  0.0 44.8 jit_solution(18410521379443379951)
XLA Ops:
  0.6 42.4 %shard_map.68 = (f32[2,4,128,128]{3,2,1,0:T(8,128)S(1)}, f32[2,8,128]{2,1,0:T(8,128)S(1)}, f32[2,2,8,128]{3,2,1,0:T(8,128)S(1)}, f32[8,128]{1,0:T(8,128)S(1)}) custom-call(bf16[256,128]{1,0:T(8,128)(2,1)} %bitcast.5, bf16[512,128]{1,0:T(8,128)(2,1)} %bitcast.4, s32[8,128]{1,0:T(8,128)} %bitcast.6, s32[8,128]{1,0:T(8,128)} %bitcast.7, s32[8,512,128]{2,1,0:T(8,128)} %cells_hbm.1), custom_call_target="tpu_custom_call" | custom-call | tf_op jit(solution)/shard_map/pallas_call | solution.py:374
  43.0 1.8 %shard_map.69 = (f32[2,512,128]{2,1,0:T(8,128)}, f32[512,128]{1,0:T(8,128)}) custom-call(f32[2,4,128,128]{3,2,1,0:T(8,128)S(1)} %get-tuple-element.6.state, f32[2,8,128]{2,1,0:T(8,128)S(1)} %get-tuple-element.7.rows_in, f32[2,2,8,128]{3,2,1,0:T(8,128)S(1)} %get-tuple-element.8.cols_in, f32[8,128]{1,0:T(8,128)S(1)} %get-tuple-element.9.rows_out), custom_call_target="tpu_custom_call" | custom-call | tf_op jit(solution)/shard_map/pallas_call | solution.py:415

commit v4 on v3

--- a/solution.py
+++ b/solution.py
@@ -28,7 +28,7 @@
 
 
 def advect_kernel(
-    base_hbm, grad_hbm, dev_hbm, block_hbm, cells_hbm, state, rows_in, cols_in, rows_out,
+    base_hbm, grad_hbm, dev_hbm, block_hbm, cells_hbm, state, rows_in, cols_in, rows_out, flow,
     base, grad, dev_ref, block_ref, cells, tab, rep, rcv, pick, sort, ask, asked, first, coef, edge_cells, edge, cols_out,
     load_sem, back_sem, send1, recv1, send2, recv2, send3, recv3, sendq, recvq, sendh, recvh,
 ):
@@ -310,6 +310,9 @@
         halo[-1].start()
     for start in range(8, GROUPS - 8, 8):
         advance_rows(start, steps)
+    for comp in range(2):
+        for q in range(GROUP_ROWS):
+            flow[comp, pl.ds(q, GROUPS, stride=GROUP_ROWS), :] = state[comp, q]
     for copies in (phase1, early, phase2, phase3, query):
         for copy in copies.values():
             copy.wait_send()
@@ -318,11 +321,8 @@
         copy.wait_recv()
 
 
-def stretch_kernel(state, rows_in, cols_in, rows_out, flow_hbm, ftle_hbm, flow, ftle, sem):
+def stretch_kernel(state, rows_in, cols_in, rows_out, flow, flow_hbm, ftle_hbm, ftle, sem):
     lat = lax.axis_index("lat")
-    for comp in range(2):
-        for q in range(GROUP_ROWS):
-            flow[comp, pl.ds(q, GROUPS, stride=GROUP_ROWS), :] = state[comp, q]
     flow_copy = pltpu.make_async_copy(flow, flow_hbm, sem.at[0])
     flow_copy.start()
     lane = lax.broadcasted_iota(jnp.int32, (GROUPS, 128), 1)
@@ -378,9 +378,10 @@
             jax.ShapeDtypeStruct((2, 8, 128), f32),
             jax.ShapeDtypeStruct((2, 2, 8, 128), f32),
             jax.ShapeDtypeStruct((8, 128), f32),
+            jax.ShapeDtypeStruct((2, 512, 128), f32),
         ),
         in_specs=[hbm] * 5,
-        out_specs=(vmem,) * 4,
+        out_specs=(vmem,) * 5,
         scratch_shapes=[
             pltpu.VMEM((256, 128), bf16),
             pltpu.VMEM((512, 128), bf16),
@@ -415,9 +416,9 @@
     return pl.pallas_call(
         stretch_kernel,
         out_shape=(jax.ShapeDtypeStruct((2, 512, 128), f32), jax.ShapeDtypeStruct((512, 128), f32)),
-        in_specs=[vmem] * 4,
+        in_specs=[vmem] * 5,
         out_specs=(hbm, hbm),
-        scratch_shapes=[pltpu.VMEM((2, 512, 128), f32), pltpu.VMEM((512, 128), f32), dma((2,))],
+        scratch_shapes=[pltpu.VMEM((512, 128), f32), dma((2,))],
         compiler_params=pltpu.CompilerParams(vmem_limit_bytes=6 << 20),
     )(*moved)
 

time: 44.9 us -> 44.7 us (level)
  no operation moved by 1% of the time
where the time goes in v4:
time: 44.7 us; the launch traced here: 44.6 us
  Pallas kernels  44 us (98%)
  between operations  0.64 us (1%)
    pallas_call x1, Pallas kernels, body(): pl.pallas_call(advect_kernel, out_shape=(jax.ShapeDtypeStruct((2, GROUP_R...  42.4 us
    pallas_call x1, Pallas kernels, body(): pl.pallas_call(stretch_kernel, out_shape=(jax.ShapeDtypeStruct((2, 512, 1...  1.61 us

profile of v4, /device:TPU:1, one launch (start us, length us, event | category | flops | bytes accessed | tf_op | source)
XLA Modules:
  0.0 44.6 jit_solution(10423981978357203262)
XLA Ops:
  0.6 42.4 %shard_map.68 = (f32[2,4,128,128]{3,2,1,0:T(8,128)S(1)}, f32[2,8,128]{2,1,0:T(8,128)S(1)}, f32[2,2,8,128]{3,2,1,0:T(8,128)S(1)}, f32[8,128]{1,0:T(8,128)S(1)}, f32[2,512,128]{2,1,0:T(8,128)S(1)}) custom-call(bf16[256,128]{1,0:T(8,128)(2,1)} %bitcast.5, bf16[512,128]{1,0:T(8,128)(2,1)} %bitcast.4, s32[8,128]{1,0:T(8,128)} %bitcast.6, s32[8,128]{1,0:T(8,128)} %bitcast.7, ...), custom_call_target="tpu_custom_call" | custom-call | tf_op jit(solution)/shard_map/pallas_call | solution.py:374
  43.0 1.6 %shard_map.69 = (f32[2,512,128]{2,1,0:T(8,128)}, f32[512,128]{1,0:T(8,128)}) custom-call(f32[2,4,128,128]{3,2,1,0:T(8,128)S(1)} %get-tuple-element.7.state, f32[2,8,128]{2,1,0:T(8,128)S(1)} %get-tuple-element.8.rows_in, f32[2,2,8,128]{3,2,1,0:T(8,128)S(1)} %get-tuple-element.9.cols_in, f32[8,128]{1,0:T(8,128)S(1)} %get-tuple-element.10.rows_out, ...), custom_call_target="tpu_custom_call" | custom-call | tf_op jit(solution)/shard_map/pallas_call | solution.py:416
